TPU v7x, 256 devices: a whole 4x4x8 slice. The times are simulated.
256 devices in a mesh: tm: 16 (over x_lo, y, core), space: 16 (over x_hi, z).
Axes of the slice: x: 4 (x_hi: 2, x_lo: 2; x = x_hi * 2 + x_lo), y: 4, z: 8, core: 2. Of those that a mesh axis runs over, the one named last changes fastest.
Arguments:
- forward_sketch: float32 [16, 8, 192, 32, 128], P('tm', None, 'space'), may hold values from -8 to 8
- adjoint_sketch: float32 [16, 8, 192, 32, 128], P('tm', None, 'space'), may hold values from -8 to 8
- coefficients: float32 [16, 4, 192, 32, 128], P('tm', None, 'space'), may hold values from -0.15 to 0.15
Outputs:
- forward_basis: float32 [16, 8, 192, 32, 128], P('tm', None, 'space')
- adjoint_basis: float32 [16, 8, 192, 32, 128], P('tm', None, 'space')
- forward_factor: float32 [16, 8, 8], P('tm')
- adjoint_factor: float32 [16, 8, 8], P('tm')
All inputs are finite; a program needn't handle non-finite values.
Results may differ from a plain program's by a relative error of at most 0.00011.
Values sent between devices are 32-bit elements; how exact they have to be, the bound alone decides.
No kernel may reach another device: no remote copies, remote signals or barrier semaphores. Data moves between devices by JAX's collectives and lax.ppermute only.
A program may use at most 64 MiB of HBM per device.

v0:
```python
import jax
import jax.numpy as jnp
from jax import lax
from jax.experimental import pallas as pl
from jax.experimental.pallas import tpu as pltpu
from jax.sharding import PartitionSpec as P

diffusion = 0.15
K, NXL, NY, NZ = 8, 12, 32, 128
PAD, TALL = 8, 48
PAIRS = [(i, j) for i in range(K) for j in range(i + 1)]
NP = len(PAIRS)
GROWS = 40
F32 = jnp.float32
ANY = pl.BlockSpec(memory_space=pltpu.HBM)
VM = pl.BlockSpec(memory_space=pltpu.VMEM)
PARAMS = pltpu.CompilerParams(vmem_limit_bytes=24 * 1024 * 1024)
COLS = (32, 25)


def sds(*shape):
    return jax.ShapeDtypeStruct(shape, F32)


def vmem(*shape):
    return pltpu.VMEM(shape, F32)


def resident(x):
    return pltpu.with_memory_space_constraint(x, pltpu.VMEM)


def rows(t, dy=0):
    return pl.ds(PAD + 8 * t + dy, 8)


BODY = pl.ds(PAD, NY)


def plane_step(adjoint, coef, src, dst):
    for t in range(NY // 8):
        here = (1.0 - 6.0 * diffusion) - coef(3, 0, rows(t))
        bz = coef(2, 0, rows(t))
        if adjoint:
            xp, xm = diffusion + coef(0, 1, rows(t)), diffusion - coef(0, -1, rows(t))
            yp, ym = diffusion + coef(1, 0, rows(t, 1)), diffusion - coef(1, 0, rows(t, -1))
            zp, zm = diffusion + pltpu.roll(bz, NZ - 1, 1), diffusion - pltpu.roll(bz, 1, 1)
        else:
            bx, by = coef(0, 0, rows(t)), coef(1, 0, rows(t))
            xp, xm = diffusion - bx, diffusion + bx
            yp, ym = diffusion - by, diffusion + by
            zp, zm = diffusion - bz, diffusion + bz
        for f in range(K):
            v = src(f, 0, rows(t))
            x = xp * src(f, 1, rows(t)) + xm * src(f, -1, rows(t))
            y = yp * src(f, 0, rows(t, 1)) + ym * src(f, 0, rows(t, -1))
            z = zp * pltpu.roll(v, NZ - 1, 1) + zm * pltpu.roll(v, 1, 1)
            dst(f, t, (here * v + x) + (y + z))


def add_gram(acc, planes):
    for p, (i, j) in enumerate(PAIRS):
        total = None
        for fields in planes:
            for t in range(NY // 8):
                prod = fields(i, t) * fields(j, t)
                total = prod if total is None else total + prod
        acc[p] += total


def zero_walls(*refs):
    for ref in refs:
        lead = ref.shape[:-2]
        ref[..., pl.ds(0, PAD), :] = jnp.zeros((*lead, PAD, NZ), F32)
        ref[..., pl.ds(PAD + NY, PAD), :] = jnp.zeros((*lead, PAD, NZ), F32)


class Copies:
    def __init__(self, sem):
        self.sem, self.count = sem, 0

    def start(self, src, dst):
        c = pltpu.make_async_copy(src, dst, self.sem.at[self.count])
        self.count += 1
        c.start()
        return c


def wait(copies):
    for c in copies:
        c.wait()


def pack_kernel(fwd, adj, cf, fup, fdn, aup, adn, sem):
    c = Copies(sem)
    work = []
    for fo, ao, first, inner, outer in ((fup, aup, NXL - 3, NXL - 2, NXL - 3), (fdn, adn, 0, 0, 2)):
        for field, out in ((fwd, fo), (adj, ao)):
            for f in range(K):
                work.append(c.start(field.at[f, pl.ds(first, 3)], out.at[pl.ds(f * 3, 3)]))
        for q in range(4):
            work.append(c.start(cf.at[q, pl.ds(inner, 2)], fo.at[pl.ds(24 + 2 * q, 2)]))
        work.append(c.start(cf.at[0, pl.ds(outer, 1)], ao.at[pl.ds(24, 1)]))
    wait(work)


def pack(fwd, adj, cf):
    return pl.pallas_call(
        pack_kernel,
        out_shape=tuple(vmem(n, NY, NZ) for n in (COLS[0], COLS[0], COLS[1], COLS[1])),
        in_specs=[ANY, ANY, ANY],
        out_specs=(VM,) * 4,
        scratch_shapes=[pltpu.SemaphoreType.DMA((42,))],
        compiler_params=PARAMS,
        name="pack",
    )(fwd, adj, cf)


def interior_kernel(fwd, adj, cf, fblock, ablock, fedge, aedge, fgram, agram, fraw, araw, cw, s1, s2, sem):
    c = Copies(sem)
    ready = [
        [c.start(cf, cw.at[:, :, BODY]), c.start(fwd, fraw.at[:, :, BODY])],
        [c.start(adj, araw.at[:, :, BODY])],
    ]
    zero_walls(fraw, araw, cw, s1, s2)
    for s, (raw, block, edge, gram) in enumerate(((fraw, fblock, fedge, fgram), (araw, ablock, aedge, agram))):
        wait(ready[s])
        for stage, (lo, hi) in enumerate(((1, 11), (2, 10), (3, 9))):
            src = (raw, s1, s2)[stage]
            dst = (s1, s2, block)[stage]

            def body(h, carry, s=s, stage=stage, lo=lo, src=src, dst=dst):
                for u in range(2):
                    p = lo + 2 * h + u

                    def put(f, t, value, p=p):
                        if stage < 2:
                            dst[f, p, rows(t)] = value
                        else:
                            dst[f, p, pl.ds(8 * t, 8)] = value

                    plane_step(
                        s == 1,
                        lambda q, dp, r, p=p: cw[q, p + dp, r],
                        lambda f, dp, r, p=p: src[f, p + dp, r],
                        put,
                    )
                return carry

            lax.fori_loop(0, (hi - lo) // 2, body, 0)
        copies = []
        for k, (ref, p) in enumerate(((s1, 1), (s1, 9), (s2, 2), (s2, 8))):
            copies.append(c.start(ref.at[:, pl.ds(p, 2), BODY], edge.at[k]))
        gram[...] = jnp.zeros((NP, 8, NZ), F32)

        def body(h, carry, block=block, gram=gram):
            add_gram(gram, [lambda f, t, p=3 + 2 * h + u: block[f, p, pl.ds(8 * t, 8)] for u in range(2)])
            return carry

        lax.fori_loop(0, 3, body, 0)
        wait(copies)


def interior(fwd, adj, cf):
    tall = pltpu.VMEM((K, NXL, TALL, NZ), F32)
    return pl.pallas_call(
        interior_kernel,
        out_shape=(
            vmem(K, NXL, NY, NZ),
            vmem(K, NXL, NY, NZ),
            vmem(4, K, 2, NY, NZ),
            vmem(4, K, 2, NY, NZ),
            vmem(NP, 8, NZ),
            vmem(NP, 8, NZ),
        ),
        in_specs=[ANY, ANY, ANY],
        out_specs=(VM,) * 6,
        scratch_shapes=[
            tall,
            tall,
            pltpu.VMEM((4, NXL, TALL, NZ), F32),
            tall,
            tall,
            pltpu.SemaphoreType.DMA((16,)),
        ],
        compiler_params=PARAMS,
        name="interior",
    )(fwd, adj, cf)


def edges_kernel(adjoint, *refs):
    if adjoint:
        field, cf, _, edge, gin, cup, cdn, up, dn, block, gout, raw, cw, s1, s2, gram, sem = refs
    else:
        field, cf, _, edge, gin, up, dn, block, gout, raw, cw, s1, s2, gram, sem = refs
        cup, cdn = up, dn
    c = Copies(sem)
    first = [
        c.start(cf.at[:, pl.ds(0, 4)], cw.at[0, :, pl.ds(3, 4), BODY]),
        c.start(cf.at[:, pl.ds(8, 4)], cw.at[1, :, pl.ds(0, 4), BODY]),
        c.start(field.at[:, pl.ds(0, 2)], raw.at[0, :, pl.ds(3, 2), BODY]),
        c.start(field.at[:, pl.ds(10, 2)], raw.at[1, :, pl.ds(0, 2), BODY]),
    ]
    for q in range(4):
        first.append(c.start(cup.at[pl.ds(24 + 2 * q, 2)], cw.at[0, q, pl.ds(1, 2), BODY]))
        first.append(c.start(cdn.at[pl.ds(24 + 2 * q, 2)], cw.at[1, q, pl.ds(4, 2), BODY]))
    if adjoint:
        first.append(c.start(up.at[pl.ds(24, 1)], cw.at[0, 0, pl.ds(0, 1), BODY]))
        first.append(c.start(dn.at[pl.ds(24, 1)], cw.at[1, 0, pl.ds(6, 1), BODY]))
    for f in range(K):
        first.append(c.start(up.at[pl.ds(f * 3, 3)], raw.at[0, f, pl.ds(0, 3), BODY]))
        first.append(c.start(dn.at[pl.ds(f * 3, 3)], raw.at[1, f, pl.ds(2, 3), BODY]))
    later = [
        c.start(edge.at[0], s1.at[0, :, pl.ds(3, 2), BODY]),
        c.start(edge.at[1], s1.at[1, :, pl.ds(0, 2), BODY]),
        c.start(edge.at[2], s2.at[0, :, pl.ds(3, 2), BODY]),
        c.start(edge.at[3], s2.at[1, :, pl.ds(0, 2), BODY]),
    ]
    zero_walls(raw, cw, s1, s2)
    gram[...] = gin[...]
    wait(first)
    for stage in (1, 2, 3):
        src, dst = ((raw, s1), (s1, s2), (s2, block))[stage - 1]

        def body(side, carry, stage=stage, src=src, dst=dst):
            for j in range(3):
                center = j + stage + side * (4 - 2 * stage)

                def put(f, t, value, j=j):
                    if stage < 3:
                        dst[side, f, j + side * 2, rows(t)] = value
                    else:
                        dst[f, j + side * 9, pl.ds(8 * t, 8)] = value

                plane_step(
                    adjoint,
                    lambda q, dp, r, center=center: cw[side, q, center + dp, r],
                    lambda f, dp, r, j=j: src[side, f, j + 1 + dp, r],
                    put,
                )
            return carry

        lax.fori_loop(0, 2, body, 0)
        if stage == 1:
            wait(later)

    def body(side, carry):
        add_gram(gram, [lambda f, t, p=side * 9 + j: block[f, p, pl.ds(8 * t, 8)] for j in range(3)])
        return carry

    lax.fori_loop(0, 2, body, 0)
    gout[pl.ds(0, NP)] = jnp.sum(gram[...], axis=1) * (1.0 / (NXL * NY * NZ * 16))
    gout[pl.ds(NP, GROWS - NP)] = jnp.zeros((GROWS - NP, NZ), F32)


def edges(adjoint, field, cf, block, edge, gram, halos):
    window = pltpu.VMEM((2, K, 5, TALL, NZ), F32)
    return pl.pallas_call(
        lambda *refs: edges_kernel(adjoint, *refs),
        out_shape=(vmem(K, NXL, NY, NZ), vmem(GROWS, NZ)),
        in_specs=[ANY, ANY] + [VM] * (3 + len(halos)),
        out_specs=(VM, VM),
        scratch_shapes=[
            window,
            pltpu.VMEM((2, 4, 7, TALL, NZ), F32),
            window,
            window,
            pltpu.VMEM((NP, 8, NZ), F32),
            pltpu.SemaphoreType.DMA((34,)),
        ],
        input_output_aliases={2: 0},
        compiler_params=PARAMS,
        name="adjoint_edges" if adjoint else "forward_edges",
    )(field, cf, block, edge, gram, *halos)


def finish_kernel(fin, ain, g0, g1, g2, g3, fout, aout, lf, la, gs, coef, fo, ao, sem):
    row = lax.broadcasted_iota(jnp.int32, (K, NZ), 0)
    lane = lax.broadcasted_iota(jnp.int32, (K, NZ), 1)
    gs[0] = jnp.broadcast_to(jnp.sum(g0[...] + g1[...], axis=1, keepdims=True), (GROWS, NZ))
    gs[1] = jnp.broadcast_to(jnp.sum(g2[...] + g3[...], axis=1, keepdims=True), (GROWS, NZ))
    for s, ref in enumerate((lf, la)):
        a = {ij: jnp.broadcast_to(gs[s, p : p + 1, :], (8, NZ)) for p, ij in enumerate(PAIRS)}
        low, diag = {}, []
        for k in range(K):
            root = jnp.sqrt(a[k, k])
            low[k, k] = root
            diag.append(1.0 / root)
            for i in range(k + 1, K):
                low[i, k] = a[i, k] * diag[k]
            for i in range(k + 1, K):
                for j in range(k + 1, i + 1):
                    a[i, j] = a[i, j] - low[i, k] * low[j, k]
        matrix = jnp.zeros((K, NZ), F32)
        for i, j in PAIRS:
            matrix = jnp.where((row == i) & (lane == j), low[i, j], matrix)
        ref[...] = matrix[:, :K]
        inv = {}
        for j in range(K):
            inv[j, j] = diag[j]
            for i in range(j + 1, K):
                total = low[i, j] * inv[j, j]
                for m in range(j + 1, i):
                    total = total + low[i, m] * inv[m, j]
                inv[i, j] = -total * diag[i]
        for p, ij in enumerate(PAIRS):
            coef[s * NP + p] = inv[ij]
    c = Copies(sem)
    work = []
    for s, (src, dst, out) in enumerate(((fin, fo, fout), (ain, ao, aout))):
        for part in range(3):

            def body(p, carry, s=s, src=src, dst=dst):
                for t in range(NY // 8):
                    fields = [src[f, p, pl.ds(8 * t, 8)] for f in range(K)]
                    for i in range(K):
                        base = s * NP + i * (i + 1) // 2
                        total = coef[base] * fields[0]
                        for j in range(1, i + 1):
                            total = total + coef[base + j] * fields[j]
                        dst[i, p, pl.ds(8 * t, 8)] = total
                return carry

            lax.fori_loop(4 * part, 4 * part + 4, body, 0)
            planes = pl.ds(4 * part, 4)
            work.append(c.start(dst.at[:, planes], out.at[:, planes]))
    wait(work)


def finish(fin, ain, grams):
    block = pltpu.VMEM((K, NXL, NY, NZ), F32)
    shape = sds(K, NXL, NY, NZ)
    return pl.pallas_call(
        finish_kernel,
        out_shape=(shape, shape, sds(K, K), sds(K, K)),
        in_specs=[VM] * 6,
        out_specs=(ANY, ANY, VM, VM),
        scratch_shapes=[
            pltpu.VMEM((2, GROWS, NZ), F32),
            pltpu.VMEM((2 * NP, 8, NZ), F32),
            block,
            block,
            pltpu.SemaphoreType.DMA((6,)),
        ],
        compiler_params=PARAMS,
        name="finish",
    )(fin, ain, *grams)


def per_device(forward_sketch, adjoint_sketch, coefficients):
    peers, slices = lax.axis_size("space"), lax.axis_size("tm")
    fwd, adj, cf = forward_sketch[0], adjoint_sketch[0], coefficients[0]
    ring = [(i, (i + 1) % peers) for i in range(peers)]
    back = [(j, i) for i, j in ring]
    later = [(i, (i + 1) % slices) for i in range(slices)]
    earlier = [(j, i) for i, j in later]

    def hop(by, flip):
        return [
            (t * peers + s, ((t + by) % slices) * peers + (s ^ flip)) for t in range(slices) for s in range(peers)
        ]

    fup, fdn, aup, adn = pack(fwd, adj, cf)
    fup, fdn = lax.ppermute(fup, "space", ring), lax.ppermute(fdn, "space", back)
    aup, adn = lax.ppermute(aup, "space", ring), lax.ppermute(adn, "space", back)
    fup, fdn, aup, adn = resident(fup), resident(fdn), resident(aup), resident(adn)
    fblock, ablock, fedge, aedge, fgram, agram = interior(fwd, adj, cf)
    fblock, fgram = edges(False, fwd, cf, fblock, fedge, fgram, (fup, fdn))
    ablock, agram = edges(True, adj, cf, ablock, aedge, agram, (fup, fdn, aup, adn))

    fblock = lax.ppermute(fblock, "tm", later)
    ablock = lax.ppermute(ablock, "tm", earlier)
    gram = jnp.concatenate([fgram, agram])
    for d in (1, 2, 4):
        gram = gram + lax.ppermute(gram, "space", [(i, i ^ d) for i in range(peers)])
    grams = [
        lax.ppermute(half, ("tm", "space"), hop(by, flip))
        for half, by in ((gram[:GROWS], 1), (gram[GROWS:], -1))
        for flip in (0, 8)
    ]
    outs = finish(resident(fblock), resident(ablock), [resident(g) for g in grams])
    return tuple(o[None] for o in outs)


def solution(mesh):
    spec = P("tm", None, "space", None, None)
    return jax.shard_map(
        per_device,
        mesh=mesh,
        in_specs=(spec, spec, spec),
        out_specs=(spec, spec, P("tm", None, None), P("tm", None, None)),
        check_vma=False,
    )
```

profile of v0, /device:TPU:2, one launch (start us, length us, event | category | flops | bytes accessed | tf_op | source)
XLA Modules:
  0.0 71.8 jit_solution(9922044456421010209)
XLA Ops:
  0.6 0.0 copy-start
  0.6 1.4 %copy-done = f32[1,8,12,32,128]{4,3,2,1,0:T(8,128)S(1)} copy-done((f32[1,8,12,32,128]{4,3,2,1,0:T(8,128)S(1)}, f32[1,8,12,32,128]{4,3,2,1,0:T(8,128)}, u32[]{:S(2)}) %copy-start) | copy-done | bytes 1572888
  2.0 0.0 copy-start.1
  2.0 1.4 %copy-done.1 = f32[1,8,12,32,128]{4,3,2,1,0:T(8,128)S(1)} copy-done((f32[1,8,12,32,128]{4,3,2,1,0:T(8,128)S(1)}, f32[1,8,12,32,128]{4,3,2,1,0:T(8,128)}, u32[]{:S(2)}) %copy-start.1) | copy-done | bytes 1572888
  3.4 0.0 copy-start.3
  3.4 1.1 %copy-done.3 = f32[1,4,12,32,128]{4,3,2,1,0:T(8,128)S(1)} copy-done((f32[1,4,12,32,128]{4,3,2,1,0:T(8,128)S(1)}, f32[1,4,12,32,128]{4,3,2,1,0:T(8,128)}, u32[]{:S(2)}) %copy-start.3) | copy-done | bytes 786456
  4.6 2.8 %pack.1 = (f32[32,32,128]{2,1,0:T(8,128)S(1)}, f32[32,32,128]{2,1,0:T(8,128)S(1)}, f32[25,32,128]{2,1,0:T(8,128)S(1)}, f32[25,32,128]{2,1,0:T(8,128)S(1)}) custom-call(f32[8,12,32,128]{3,2,1,0:T(8,128)S(1)} %bitcast.7, f32[8,12,32,128]{3,2,1,0:T(8,128)S(1)} %bitcast.10, f32[4,12,32,128]{3,2,1,0:T(8,128)S(1)} %bitcast.13), custom_call_target="tpu_custom_call" | custom-call | tf_op jit(solution)/shard_map/pack/pallas_call | solution.py:108
  7.4 2.0 %collective-permute-start = (f32[32,32,128]{2,1,0:T(8,128)S(1)}, f32[32,32,128]{2,1,0:T(8,128)S(1)}, u32[]{:S(2)}, u32[]{:S(2)}) collective-permute-start(f32[32,32,128]{2,1,0:T(8,128)S(1)} %get-tuple-element.25), channel_id=1, source_target_pairs={{0,1},{1,2},{2,3},{3,4},{4,5},{5,6},{6,7},{7,8},{8,9},{9,10},{10,1... | collective-permute-start | bytes 1572872 | tf_op jit(solution)/shard_map/ppermute | solution.py:364
  9.4 5.6 %collective-permute-start.1 = (f32[32,32,128]{2,1,0:T(8,128)S(1)}, f32[32,32,128]{2,1,0:T(8,128)S(1)}, u32[]{:S(2)}, u32[]{:S(2)}) collective-permute-start(f32[32,32,128]{2,1,0:T(8,128)S(1)} %get-tuple-element.26), channel_id=1, source_target_pairs={{1,0},{2,1},{3,2},{4,3},{5,4},{6,5},{7,6},{8,7},{9,8},{10,9},{11,1... | collective-permute-start | bytes 1572872 | tf_op jit(solution)/shard_map/ppermute | solution.py:364
  15.0 0.0 collective-permute-start.3
  15.0 0.0 copy-start.4
  15.0 5.6 %collective-permute-start.4 = (f32[25,32,128]{2,1,0:T(8,128)S(1)}, f32[25,32,128]{2,1,0:T(8,128)S(1)}, u32[]{:S(2)}, u32[]{:S(2)}) collective-permute-start(f32[25,32,128]{2,1,0:T(8,128)S(1)} %get-tuple-element.32), channel_id=1, source_target_pairs={{1,0},{2,1},{3,2},{4,3},{5,4},{6,5},{7,6},{8,7},{9,8},{10,9},{11,1... | collective-permute-start | bytes 1228808 | tf_op jit(solution)/shard_map/ppermute | solution.py:365
  20.6 6.7 %interior.1 = (f32[8,12,32,128]{3,2,1,0:T(8,128)S(1)}, f32[8,12,32,128]{3,2,1,0:T(8,128)S(1)}, f32[4,8,2,32,128]{4,3,2,1,0:T(8,128)S(1)}, f32[4,8,2,32,128]{4,3,...) custom-call(f32[8,12,32,128]{3,2,1,0:T(8,128)S(1)} %bitcast.8, f32[8,12,32,128]{3,2,1,0:T(8,128)S(1)} %bitcast.11, ...), custom_call_target="tpu_custom_call" | custom-call | tf_op jit(solution)/shard_map/interior/pallas_call | solution.py:166
  27.3 0.4 collective-permute-done.refs_5_
  27.7 0.0 collective-permute-done.1.refs_6_
  27.7 0.0 copy-done.4
  27.7 0.0 copy-start.2
  27.7 3.1 %forward_edges.1 = (f32[8,12,32,128]{3,2,1,0:T(8,128)S(1)}, f32[40,128]{1,0:T(8,128)S(1)}) custom-call(f32[8,12,32,128]{3,2,1,0:T(8,128)S(1)} %bitcast.9, f32[4,12,32,128]{3,2,1,0:T(8,128)S(1)} %bitcast.15, f32[8,12,32,128]{3,2,1,0:T(8,128)S(1)} %get-tuple-element.22.refs_2_, ...), custom_call_target="tpu_custom_call", output_to_operand_aliasing={{0}: (2, {})} | custom-call | tf_op jit(solution)/shard_map/forward_edges/pallas_call | solution.py:258
  30.8 0.1 collective-permute-start.2
  30.9 4.7 %collective-permute-done.3.refs_7_ = f32[25,32,128]{2,1,0:T(8,128)S(1)} collective-permute-done((f32[25,32,128]{2,1,0:T(8,128)S(1)}, f32[25,32,128]{2,1,0:T(8,128)S(1)}, u32[]{:S(2)}, u32[]{:S(2)}) %collective-permute-start.3) | collective-permute-done | bytes 409632 | tf_op jit(solution)/shard_map/ppermute | solution.py:365
  35.6 0.0 collective-permute-done.4.refs_8_
  35.6 0.0 copy-done.2
  35.6 3.3 %adjoint_edges.1 = (f32[8,12,32,128]{3,2,1,0:T(8,128)S(1)}, f32[40,128]{1,0:T(8,128)S(1)}) custom-call(f32[8,12,32,128]{3,2,1,0:T(8,128)S(1)} %bitcast.12, f32[4,12,32,128]{3,2,1,0:T(8,128)S(1)} %bitcast.16, f32[8,12,32,128]{3,2,1,0:T(8,128)S(1)} %get-tuple-element.28.refs_2_, ...), custom_call_target="tpu_custom_call", output_to_operand_aliasing={{0}: (2, {})} | custom-call | tf_op jit(solution)/shard_map/adjoint_edges/pallas_call | solution.py:258
  38.9 2.8 %collective-permute-start.5 = (f32[8,12,32,128]{3,2,1,0:T(8,128)S(1)}, f32[8,12,32,128]{3,2,1,0:T(8,128)S(1)}, u32[]{:S(2)}, u32[]{:S(2)}) collective-permute-start(f32[8,12,32,128]{3,2,1,0:T(8,128)S(1)} %get-tuple-element.33), channel_id=1, source_target_pairs={{16,0},{32,16},{48,32},{64,48},{80,64},{96,80},{112,96},{128,112},... | collective-permute-start | bytes 4718600 | tf_op jit(solution)/shard_map/ppermute | solution.py:372
  41.8 0.0 collective-permute-start.6
  41.8 4.0 %collective-permute-done.6 = f32[80,128]{1,0:T(8,128)S(1)} collective-permute-done((f32[80,128]{1,0:T(8,128)S(1)}, f32[80,128]{1,0:T(8,128)S(1)}, u32[]{:S(2)}, u32[]{:S(2)}) %collective-permute-start.6) | collective-permute-done | bytes 40992 | tf_op jit(solution)/shard_map/ppermute | solution.py:375
  45.8 0.1 collective-permute-start.7
  45.9 4.8 %collective-permute-done.7 = f32[80,128]{1,0:T(8,128)S(1)} collective-permute-done((f32[80,128]{1,0:T(8,128)S(1)}, f32[80,128]{1,0:T(8,128)S(1)}, u32[]{:S(2)}, u32[]{:S(2)}) %collective-permute-start.7) | collective-permute-done | bytes 40992 | tf_op jit(solution)/shard_map/ppermute | solution.py:375
  50.7 1.6 %collective-permute-start.8 = (f32[80,128]{1,0:T(8,128)S(1)}, f32[80,128]{1,0:T(8,128)S(1)}, u32[]{:S(2)}, u32[]{:S(2)}) collective-permute-start(f32[80,128]{1,0:T(8,128)S(1)} %add.10), channel_id=1, source_target_pairs={{0,4},{1,5},{2,6},{3,7},{4,0},{5,1},{6,2},{7,3},{8,12},{9,13},{10,... | collective-permute-start | bytes 122888 | tf_op jit(solution)/shard_map/ppermute | solution.py:375
  52.3 6.3 %collective-permute-done.8 = f32[80,128]{1,0:T(8,128)S(1)} collective-permute-done((f32[80,128]{1,0:T(8,128)S(1)}, f32[80,128]{1,0:T(8,128)S(1)}, u32[]{:S(2)}, u32[]{:S(2)}) %collective-permute-start.8) | collective-permute-done | bytes 40992 | tf_op jit(solution)/shard_map/ppermute | solution.py:375
  58.6 0.3 collective-permute-start.12
  58.9 2.3 %collective-permute-start.11 = (f32[40,128]{1,0:T(8,128)S(1)}, f32[40,128]{1,0:T(8,128)S(1)}, u32[]{:S(2)}, u32[]{:S(2)}) collective-permute-start(f32[40,128]{1,0:T(8,128)S(1)} %get-tuple-element.40), channel_id=1, source_target_pairs={{0,240},{1,241},{2,242},{3,243},{4,244},{5,245},{6,246},{7,247},{8... | collective-permute-start | bytes 61448 | tf_op jit(solution)/shard_map/ppermute | solution.py:377
  61.2 0.9 %collective-permute-start.10 = (f32[40,128]{1,0:T(8,128)S(1)}, f32[40,128]{1,0:T(8,128)S(1)}, u32[]{:S(2)}, u32[]{:S(2)}) collective-permute-start(f32[40,128]{1,0:T(8,128)S(1)} %get-tuple-element.41), channel_id=1, source_target_pairs={{0,24},{1,25},{2,26},{3,27},{4,28},{5,29},{6,30},{7,31},{8,16},{9,... | collective-permute-start | bytes 61448 | tf_op jit(solution)/shard_map/ppermute | solution.py:377
  62.1 1.5 %collective-permute-done.12.g3 = f32[40,128]{1,0:T(8,128)S(1)} collective-permute-done((f32[40,128]{1,0:T(8,128)S(1)}, f32[40,128]{1,0:T(8,128)S(1)}, u32[]{:S(2)}, u32[]{:S(2)}) %collective-permute-start.12) | collective-permute-done | bytes 20512 | tf_op jit(solution)/shard_map/ppermute | solution.py:377
  63.6 0.1 collective-permute-start.9
  63.7 0.0 collective-permute-done.11.g2
  63.7 2.8 %collective-permute-done.10.g1 = f32[40,128]{1,0:T(8,128)S(1)} collective-permute-done((f32[40,128]{1,0:T(8,128)S(1)}, f32[40,128]{1,0:T(8,128)S(1)}, u32[]{:S(2)}, u32[]{:S(2)}) %collective-permute-start.10) | collective-permute-done | bytes 20512 | tf_op jit(solution)/shard_map/ppermute | solution.py:377
  66.5 2.4 %collective-permute-done.9.g0 = f32[40,128]{1,0:T(8,128)S(1)} collective-permute-done((f32[40,128]{1,0:T(8,128)S(1)}, f32[40,128]{1,0:T(8,128)S(1)}, u32[]{:S(2)}, u32[]{:S(2)}) %collective-permute-start.9) | collective-permute-done | bytes 20512 | tf_op jit(solution)/shard_map/ppermute | solution.py:377
  68.9 0.0 collective-permute-done.2.fin
  68.9 0.0 collective-permute-done.5.ain
  68.9 2.8 %finish.1 = (f32[8,12,32,128]{3,2,1,0:T(8,128)}, f32[8,12,32,128]{3,2,1,0:T(8,128)}, f32[8,8]{1,0:T(8,128)}, f32[8,8]{1,0:T(8,128)}) custom-call(f32[8,12,32,128]{3,2,1,0:T(8,128)S(1)} %collective-permute-done.2.fin, f32[8,12,32,128]{3,2,1,0:T(8,128)S(1)} %collective-permute-done.5.ain, f32[40,128]{1,0:T(8,128)S(1)} %collective-permute-done.9.g0, ...), custom_call_target="tpu_custom_call" | custom-call | tf_op jit(solution)/shard_map/finish/pallas_call | solution.py:333
  (6 shorter events, 0.0 us)
Async XLA Ops:
  0.6 1.4 %copy-start = (f32[1,8,12,32,128]{4,3,2,1,0:T(8,128)S(1)}, f32[1,8,12,32,128]{4,3,2,1,0:T(8,128)}, u32[]{:S(2)}) copy-start(f32[1,8,12,32,128]{4,3,2,1,0:T(8,128)} %param.3) | copy-start | bytes 4718596
  2.0 1.4 %copy-start.1 = (f32[1,8,12,32,128]{4,3,2,1,0:T(8,128)S(1)}, f32[1,8,12,32,128]{4,3,2,1,0:T(8,128)}, u32[]{:S(2)}) copy-start(f32[1,8,12,32,128]{4,3,2,1,0:T(8,128)} %param.4) | copy-start | bytes 4718596
  3.4 1.1 %copy-start.3 = (f32[1,4,12,32,128]{4,3,2,1,0:T(8,128)S(1)}, f32[1,4,12,32,128]{4,3,2,1,0:T(8,128)}, u32[]{:S(2)}) copy-start(f32[1,4,12,32,128]{4,3,2,1,0:T(8,128)} %param.5) | copy-start | bytes 2359300
  7.4 20.3 %collective-permute-start = (f32[32,32,128]{2,1,0:T(8,128)S(1)}, f32[32,32,128]{2,1,0:T(8,128)S(1)}, u32[]{:S(2)}, u32[]{:S(2)}) collective-permute-start(f32[32,32,128]{2,1,0:T(8,128)S(1)} %get-tuple-element.25), channel_id=1, source_target_pairs={{0,1},{1,2},{2,3},{3,4},{4,5},{5,6},{6,7},{7,8},{8,9},{9,10},{10,1... | collective-permute-start | bytes 1572872 | tf_op jit(solution)/shard_map/ppermute | solution.py:364
  9.4 18.3 %collective-permute-start.1 = (f32[32,32,128]{2,1,0:T(8,128)S(1)}, f32[32,32,128]{2,1,0:T(8,128)S(1)}, u32[]{:S(2)}, u32[]{:S(2)}) collective-permute-start(f32[32,32,128]{2,1,0:T(8,128)S(1)} %get-tuple-element.26), channel_id=1, source_target_pairs={{1,0},{2,1},{3,2},{4,3},{5,4},{6,5},{7,6},{8,7},{9,8},{10,9},{11,1... | collective-permute-start | bytes 1572872 | tf_op jit(solution)/shard_map/ppermute | solution.py:364
  15.0 20.6 %collective-permute-start.3 = (f32[25,32,128]{2,1,0:T(8,128)S(1)}, f32[25,32,128]{2,1,0:T(8,128)S(1)}, u32[]{:S(2)}, u32[]{:S(2)}) collective-permute-start(f32[25,32,128]{2,1,0:T(8,128)S(1)} %get-tuple-element.31), channel_id=1, source_target_pairs={{0,1},{1,2},{2,3},{3,4},{4,5},{5,6},{6,7},{7,8},{8,9},{9,10},{10,1... | collective-permute-start | bytes 1228808 | tf_op jit(solution)/shard_map/ppermute | solution.py:365
  15.0 12.7 %copy-start.4 = (f32[1,4,12,32,128]{4,3,2,1,0:T(8,128)S(1)}, f32[1,4,12,32,128]{4,3,2,1,0:T(8,128)}, u32[]{:S(2)}) copy-start(f32[1,4,12,32,128]{4,3,2,1,0:T(8,128)} %param.5) | copy-start | bytes 2359300
  15.0 20.6 %collective-permute-start.4 = (f32[25,32,128]{2,1,0:T(8,128)S(1)}, f32[25,32,128]{2,1,0:T(8,128)S(1)}, u32[]{:S(2)}, u32[]{:S(2)}) collective-permute-start(f32[25,32,128]{2,1,0:T(8,128)S(1)} %get-tuple-element.32), channel_id=1, source_target_pairs={{1,0},{2,1},{3,2},{4,3},{5,4},{6,5},{7,6},{8,7},{9,8},{10,9},{11,1... | collective-permute-start | bytes 1228808 | tf_op jit(solution)/shard_map/ppermute | solution.py:365
  27.7 7.9 %copy-start.2 = (f32[1,8,12,32,128]{4,3,2,1,0:T(8,128)S(1)}, f32[1,8,12,32,128]{4,3,2,1,0:T(8,128)}, u32[]{:S(2)}) copy-start(f32[1,8,12,32,128]{4,3,2,1,0:T(8,128)} %param.4) | copy-start | bytes 4718596
  30.8 38.1 %collective-permute-start.2 = (f32[8,12,32,128]{3,2,1,0:T(8,128)S(1)}, f32[8,12,32,128]{3,2,1,0:T(8,128)S(1)}, u32[]{:S(2)}, u32[]{:S(2)}) collective-permute-start(f32[8,12,32,128]{3,2,1,0:T(8,128)S(1)} %get-tuple-element.27), channel_id=1, source_target_pairs={{0,16},{16,32},{32,48},{48,64},{64,80},{80,96},{96,112},{112,128},... | collective-permute-start | bytes 4718600 | tf_op jit(solution)/shard_map/ppermute | solution.py:371
  38.9 30.0 %collective-permute-start.5 = (f32[8,12,32,128]{3,2,1,0:T(8,128)S(1)}, f32[8,12,32,128]{3,2,1,0:T(8,128)S(1)}, u32[]{:S(2)}, u32[]{:S(2)}) collective-permute-start(f32[8,12,32,128]{3,2,1,0:T(8,128)S(1)} %get-tuple-element.33), channel_id=1, source_target_pairs={{16,0},{32,16},{48,32},{64,48},{80,64},{96,80},{112,96},{128,112},... | collective-permute-start | bytes 4718600 | tf_op jit(solution)/shard_map/ppermute | solution.py:372
  41.8 4.0 %collective-permute-start.6 = (f32[80,128]{1,0:T(8,128)S(1)}, f32[80,128]{1,0:T(8,128)S(1)}, u32[]{:S(2)}, u32[]{:S(2)}) collective-permute-start(f32[80,128]{1,0:T(8,128)S(1)} %constant_dynamic-update-slice_fusion), channel_id=1, source_target_pairs={{0,1},{1,0},{2,3},{3,2},{4,5},{5,4},{6,7},{7,6},{8,9},{9,8},{10,11... | collective-permute-start | bytes 122888 | tf_op jit(solution)/shard_map/ppermute | solution.py:375
  45.8 4.9 %collective-permute-start.7 = (f32[80,128]{1,0:T(8,128)S(1)}, f32[80,128]{1,0:T(8,128)S(1)}, u32[]{:S(2)}, u32[]{:S(2)}) collective-permute-start(f32[80,128]{1,0:T(8,128)S(1)} %add.9), channel_id=1, source_target_pairs={{0,2},{1,3},{2,0},{3,1},{4,6},{5,7},{6,4},{7,5},{8,10},{9,11},{10,... | collective-permute-start | bytes 122888 | tf_op jit(solution)/shard_map/ppermute | solution.py:375
  50.7 7.9 %collective-permute-start.8 = (f32[80,128]{1,0:T(8,128)S(1)}, f32[80,128]{1,0:T(8,128)S(1)}, u32[]{:S(2)}, u32[]{:S(2)}) collective-permute-start(f32[80,128]{1,0:T(8,128)S(1)} %add.10), channel_id=1, source_target_pairs={{0,4},{1,5},{2,6},{3,7},{4,0},{5,1},{6,2},{7,3},{8,12},{9,13},{10,... | collective-permute-start | bytes 122888 | tf_op jit(solution)/shard_map/ppermute | solution.py:375
  58.6 5.0 %collective-permute-start.12 = (f32[40,128]{1,0:T(8,128)S(1)}, f32[40,128]{1,0:T(8,128)S(1)}, u32[]{:S(2)}, u32[]{:S(2)}) collective-permute-start(f32[40,128]{1,0:T(8,128)S(1)} %get-tuple-element.40), channel_id=1, source_target_pairs={{0,248},{1,249},{2,250},{3,251},{4,252},{5,253},{6,254},{7,255},{8... | collective-permute-start | bytes 61448 | tf_op jit(solution)/shard_map/ppermute | solution.py:377
  58.9 4.8 %collective-permute-start.11 = (f32[40,128]{1,0:T(8,128)S(1)}, f32[40,128]{1,0:T(8,128)S(1)}, u32[]{:S(2)}, u32[]{:S(2)}) collective-permute-start(f32[40,128]{1,0:T(8,128)S(1)} %get-tuple-element.40), channel_id=1, source_target_pairs={{0,240},{1,241},{2,242},{3,243},{4,244},{5,245},{6,246},{7,247},{8... | collective-permute-start | bytes 61448 | tf_op jit(solution)/shard_map/ppermute | solution.py:377
  61.2 5.3 %collective-permute-start.10 = (f32[40,128]{1,0:T(8,128)S(1)}, f32[40,128]{1,0:T(8,128)S(1)}, u32[]{:S(2)}, u32[]{:S(2)}) collective-permute-start(f32[40,128]{1,0:T(8,128)S(1)} %get-tuple-element.41), channel_id=1, source_target_pairs={{0,24},{1,25},{2,26},{3,27},{4,28},{5,29},{6,30},{7,31},{8,16},{9,... | collective-permute-start | bytes 61448 | tf_op jit(solution)/shard_map/ppermute | solution.py:377
  63.6 5.3 %collective-permute-start.9 = (f32[40,128]{1,0:T(8,128)S(1)}, f32[40,128]{1,0:T(8,128)S(1)}, u32[]{:S(2)}, u32[]{:S(2)}) collective-permute-start(f32[40,128]{1,0:T(8,128)S(1)} %get-tuple-element.41), channel_id=1, source_target_pairs={{0,16},{1,17},{2,18},{3,19},{4,20},{5,21},{6,22},{7,23},{8,24},{9,... | collective-permute-start | bytes 61448 | tf_op jit(solution)/shard_map/ppermute | solution.py:377
where the time goes:
time: 72 us; the launch traced here: 71.8 us
  waiting for transfers between devices  26.9 us (37%)
  starting transfers between devices  21.4 us (30%)
  Pallas kernels  18.7 us (26%)
  local copies, waits for them, and re-layouts  3.96 us (6%)
  between operations  0.87 us (1%)
    ppermute x3, waiting for transfers between devices, per_device(): lax.ppermute(gram, 'space', [(i, i ^ d) for i in range(peers)])  15.1 us
    pallas_call x1, Pallas kernels, interior(): pl.pallas_call(interior_kernel, out_shape=(vmem(K, NXL, NY, NZ), vmem(K,...  6.67 us
    ppermute x4, waiting for transfers between devices, per_device(): lax.ppermute(half, ('tm', 'space'), hop(by, flip))  6.65 us
    pallas_call x2, Pallas kernels, edges(): pl.pallas_call(lambda *refs: edges_kernel(adjoint, *refs), out_shape=(vme...  6.42 us
    ppermute x1, starting transfers between devices, per_device(): lax.ppermute(adn, 'space', back)  5.64 us
    ppermute x1, starting transfers between devices, per_device(): lax.ppermute(fdn, 'space', back)  5.59 us
    ppermute x1, waiting for transfers between devices, per_device(): lax.ppermute(aup, 'space', ring)  4.71 us
    unnamed x11, local copies, waits for them, and re-layouts  3.95 us
  transfers between devices with their start and end apart: 13, of which 8 were waited for; matrix products, arithmetic and copies ran while one was open for 0% of the time, Pallas kernels for 18%

commit v1 on v0

--- a/solution.py
+++ b/solution.py
@@ -15,7 +15,6 @@
 ANY = pl.BlockSpec(memory_space=pltpu.HBM)
 VM = pl.BlockSpec(memory_space=pltpu.VMEM)
 PARAMS = pltpu.CompilerParams(vmem_limit_bytes=24 * 1024 * 1024)
-COLS = (32, 25)
 
 
 def sds(*shape):
@@ -91,29 +90,59 @@
         c.wait()
 
 
-def pack_kernel(fwd, adj, cf, fup, fdn, aup, adn, sem):
+def parity():
+    return lax.axis_index("space") % 2
+
+
+def pack_kernel(adjoint, field, cf, *refs):
+    *outs, raw, cw, sem = refs
     c = Copies(sem)
-    work = []
-    for fo, ao, first, inner, outer in ((fup, aup, NXL - 3, NXL - 2, NXL - 3), (fdn, adn, 0, 0, 2)):
-        for field, out in ((fwd, fo), (adj, ao)):
-            for f in range(K):
-                work.append(c.start(field.at[f, pl.ds(first, 3)], out.at[pl.ds(f * 3, 3)]))
-        for q in range(4):
-            work.append(c.start(cf.at[q, pl.ds(inner, 2)], fo.at[pl.ds(24 + 2 * q, 2)]))
-        work.append(c.start(cf.at[0, pl.ds(outer, 1)], ao.at[pl.ds(24, 1)]))
-    wait(work)
-
-
-def pack(fwd, adj, cf):
+    loads, sends = [], []
+    to_next = [parity(), 1 - parity()]
+    for k, out in enumerate(outs):
+        first, inner, outer = (to_next[k] * (NXL - n) for n in (3, 2, 1))
+        loads.append(c.start(field.at[:, pl.ds(first, 3)], raw.at[k, :, :, BODY]))
+        loads.append(c.start(cf.at[:, pl.ds(first, 3)], cw.at[k, :, :, BODY]))
+        sends.append(c.start(field.at[:, pl.ds(inner, 2)], out.at[pl.ds(0, K), pl.ds(to_next[k], 2)]))
+        if out.shape[0] > K:
+            sends.append(c.start(cf.at[0, pl.ds(inner, 2)], out.at[K, pl.ds(0, 2)]))
+            sends.append(c.start(cf.at[1, outer], out.at[K, 2]))
+            sends.append(c.start(cf.at[2, outer], out.at[K + 1, 0]))
+            sends.append(c.start(cf.at[3, outer], out.at[K + 1, 1]))
+    for ref, n in ((raw, K), (cw, 4)):
+        for row in (0, PAD + NY):
+            ref[:, :, pl.ds(1, 1), pl.ds(row, PAD), :] = jnp.zeros((2, n, 1, PAD, NZ), F32)
+    wait(loads)
+    for k, out in enumerate(outs):
+        slot = 2 - 2 * to_next[k]
+
+        def put(f, t, value, out=out, slot=slot):
+            out[f, slot, pl.ds(8 * t, 8)] = value
+
+        plane_step(
+            adjoint,
+            lambda q, dp, r, k=k: cw[k, q, 1 + dp, r],
+            lambda f, dp, r, k=k: raw[k, f, 1 + dp, r],
+            put,
+        )
+    wait(sends)
+
+
+def pack(adjoint, field, cf):
+    out = vmem(K if adjoint else K + 2, 3, NY, NZ)
     return pl.pallas_call(
-        pack_kernel,
-        out_shape=tuple(vmem(n, NY, NZ) for n in (COLS[0], COLS[0], COLS[1], COLS[1])),
-        in_specs=[ANY, ANY, ANY],
-        out_specs=(VM,) * 4,
-        scratch_shapes=[pltpu.SemaphoreType.DMA((42,))],
+        lambda *refs: pack_kernel(adjoint, *refs),
+        out_shape=(out, out),
+        in_specs=[ANY, ANY],
+        out_specs=(VM, VM),
+        scratch_shapes=[
+            pltpu.VMEM((2, K, 3, TALL, NZ), F32),
+            pltpu.VMEM((2, 4, 3, TALL, NZ), F32),
+            pltpu.SemaphoreType.DMA((16,)),
+        ],
         compiler_params=PARAMS,
-        name="pack",
-    )(fwd, adj, cf)
+        name="adjoint_pack" if adjoint else "forward_pack",
+    )(field, cf)
 
 
 def interior_kernel(fwd, adj, cf, fblock, ablock, fedge, aedge, fgram, agram, fraw, araw, cw, s1, s2, sem):
@@ -190,10 +219,10 @@
 
 def edges_kernel(adjoint, *refs):
     if adjoint:
-        field, cf, _, edge, gin, cup, cdn, up, dn, block, gout, raw, cw, s1, s2, gram, sem = refs
+        field, cf, _, edge, gin, *halos = refs[:9]
     else:
-        field, cf, _, edge, gin, up, dn, block, gout, raw, cw, s1, s2, gram, sem = refs
-        cup, cdn = up, dn
+        field, cf, _, edge, gin, *halos = refs[:7]
+    block, gout, raw, cw, s1, s2, gram, sem = refs[len(refs) - 8 :]
     c = Copies(sem)
     first = [
         c.start(cf.at[:, pl.ds(0, 4)], cw.at[0, :, pl.ds(3, 4), BODY]),
@@ -201,15 +230,14 @@
         c.start(field.at[:, pl.ds(0, 2)], raw.at[0, :, pl.ds(3, 2), BODY]),
         c.start(field.at[:, pl.ds(10, 2)], raw.at[1, :, pl.ds(0, 2), BODY]),
     ]
-    for q in range(4):
-        first.append(c.start(cup.at[pl.ds(24 + 2 * q, 2)], cw.at[0, q, pl.ds(1, 2), BODY]))
-        first.append(c.start(cdn.at[pl.ds(24 + 2 * q, 2)], cw.at[1, q, pl.ds(4, 2), BODY]))
-    if adjoint:
-        first.append(c.start(up.at[pl.ds(24, 1)], cw.at[0, 0, pl.ds(0, 1), BODY]))
-        first.append(c.start(dn.at[pl.ds(24, 1)], cw.at[1, 0, pl.ds(6, 1), BODY]))
-    for f in range(K):
-        first.append(c.start(up.at[pl.ds(f * 3, 3)], raw.at[0, f, pl.ds(0, 3), BODY]))
-        first.append(c.start(dn.at[pl.ds(f * 3, 3)], raw.at[1, f, pl.ds(2, 3), BODY]))
+    for k in range(2):
+        side = parity() if k == 0 else 1 - parity()
+        shared, own = halos[k], halos[len(halos) - 2 + k]
+        first.append(c.start(own.at[pl.ds(0, K), pl.ds(1 - side, 2)], raw.at[side, :, pl.ds(1 + side, 2), BODY]))
+        first.append(c.start(own.at[pl.ds(0, K), pl.ds(2 * side, 1)], s1.at[side, :, pl.ds(4 * side, 1), BODY]))
+        first.append(c.start(shared.at[K, pl.ds(0, 2)], cw.at[side, 0, pl.ds(1 + 3 * side, 2), BODY]))
+        for q, at in enumerate(((K, 2), (K + 1, 0), (K + 1, 1))):
+            first.append(c.start(shared.at[at], cw.at[side, 1 + q, 2 + 2 * side, BODY]))
     later = [
         c.start(edge.at[0], s1.at[0, :, pl.ds(3, 2), BODY]),
         c.start(edge.at[1], s1.at[1, :, pl.ds(0, 2), BODY]),
@@ -223,7 +251,8 @@
         src, dst = ((raw, s1), (s1, s2), (s2, block))[stage - 1]
 
         def body(side, carry, stage=stage, src=src, dst=dst):
-            for j in range(3):
+            for u in range(2 if stage == 1 else 3):
+                j = u + 1 - side if stage == 1 else u
                 center = j + stage + side * (4 - 2 * stage)
 
                 def put(f, t, value, j=j):
@@ -266,7 +295,7 @@
             window,
             window,
             pltpu.VMEM((NP, 8, NZ), F32),
-            pltpu.SemaphoreType.DMA((34,)),
+            pltpu.SemaphoreType.DMA((24,)),
         ],
         input_output_aliases={2: 0},
         compiler_params=PARAMS,
@@ -274,11 +303,12 @@
     )(field, cf, block, edge, gram, *halos)
 
 
-def finish_kernel(fin, ain, g0, g1, g2, g3, fout, aout, lf, la, gs, coef, fo, ao, sem):
+def finish_kernel(fin, ain, gf, g0, g1, fout, aout, lf, la, gs, coef, fo, ao, sem):
     row = lax.broadcasted_iota(jnp.int32, (K, NZ), 0)
     lane = lax.broadcasted_iota(jnp.int32, (K, NZ), 1)
-    gs[0] = jnp.broadcast_to(jnp.sum(g0[...] + g1[...], axis=1, keepdims=True), (GROWS, NZ))
-    gs[1] = jnp.broadcast_to(jnp.sum(g2[...] + g3[...], axis=1, keepdims=True), (GROWS, NZ))
+    ga = g0[pl.ds(GROWS, GROWS)] + g1[pl.ds(GROWS, GROWS)]
+    gs[0] = jnp.broadcast_to(jnp.sum(gf[pl.ds(0, GROWS)], axis=1, keepdims=True), (GROWS, NZ))
+    gs[1] = jnp.broadcast_to(jnp.sum(ga, axis=1, keepdims=True), (GROWS, NZ))
     for s, ref in enumerate((lf, la)):
         a = {ij: jnp.broadcast_to(gs[s, p : p + 1, :], (8, NZ)) for p, ij in enumerate(PAIRS)}
         low, diag = {}, []
@@ -333,7 +363,7 @@
     return pl.pallas_call(
         finish_kernel,
         out_shape=(shape, shape, sds(K, K), sds(K, K)),
-        in_specs=[VM] * 6,
+        in_specs=[VM] * 5,
         out_specs=(ANY, ANY, VM, VM),
         scratch_shapes=[
             pltpu.VMEM((2, GROWS, NZ), F32),
@@ -349,9 +379,10 @@
 
 def per_device(forward_sketch, adjoint_sketch, coefficients):
     peers, slices = lax.axis_size("space"), lax.axis_size("tm")
-    fwd, adj, cf = forward_sketch[0], adjoint_sketch[0], coefficients[0]
-    ring = [(i, (i + 1) % peers) for i in range(peers)]
-    back = [(j, i) for i, j in ring]
+    fwd, adj, cf = (pltpu.with_memory_space_constraint(x[0], pltpu.HBM) for x in (forward_sketch, adjoint_sketch, coefficients))
+    partner = [
+        [(i, (i + 1 if (i % 2 == 1) == (k == 0) else i - 1) % peers) for i in range(peers)] for k in range(2)
+    ]
     later = [(i, (i + 1) % slices) for i in range(slices)]
     earlier = [(j, i) for i, j in later]
 
@@ -360,24 +391,19 @@
             (t * peers + s, ((t + by) % slices) * peers + (s ^ flip)) for t in range(slices) for s in range(peers)
         ]
 
-    fup, fdn, aup, adn = pack(fwd, adj, cf)
-    fup, fdn = lax.ppermute(fup, "space", ring), lax.ppermute(fdn, "space", back)
-    aup, adn = lax.ppermute(aup, "space", ring), lax.ppermute(adn, "space", back)
-    fup, fdn, aup, adn = resident(fup), resident(fdn), resident(aup), resident(adn)
+    fhalo = [lax.ppermute(x, "space", partner[k]) for k, x in enumerate(pack(False, fwd, cf))]
+    ahalo = [lax.ppermute(x, "space", partner[k]) for k, x in enumerate(pack(True, adj, cf))]
+    fhalo, ahalo = [resident(x) for x in fhalo], [resident(x) for x in ahalo]
     fblock, ablock, fedge, aedge, fgram, agram = interior(fwd, adj, cf)
-    fblock, fgram = edges(False, fwd, cf, fblock, fedge, fgram, (fup, fdn))
-    ablock, agram = edges(True, adj, cf, ablock, aedge, agram, (fup, fdn, aup, adn))
-
+    fblock, fgram = edges(False, fwd, cf, fblock, fedge, fgram, fhalo)
+    fgram = sum(lax.ppermute(fgram, ("tm", "space"), hop(1, flip)) for flip in (0, 8))
+    ablock, agram = edges(True, adj, cf, ablock, aedge, agram, fhalo + ahalo)
     fblock = lax.ppermute(fblock, "tm", later)
     ablock = lax.ppermute(ablock, "tm", earlier)
     gram = jnp.concatenate([fgram, agram])
-    for d in (1, 2, 4):
+    for d in (1, 2, 7):
         gram = gram + lax.ppermute(gram, "space", [(i, i ^ d) for i in range(peers)])
-    grams = [
-        lax.ppermute(half, ("tm", "space"), hop(by, flip))
-        for half, by in ((gram[:GROWS], 1), (gram[GROWS:], -1))
-        for flip in (0, 8)
-    ]
+    grams = [gram] + [lax.ppermute(gram, ("tm", "space"), hop(-1, flip)) for flip in (0, 8)]
     outs = finish(resident(fblock), resident(ablock), [resident(g) for g in grams])
     return tuple(o[None] for o in outs)
 

time: 72 us -> 87.5 us (1.22)
  the two profiles are of different devices: /device:TPU:2 before, /device:TPU:1 now
where the time goes in v1:
time: 87.5 us; the launch traced here: 87.3 us
  waiting for transfers between devices  38.2 us (44%)
  starting transfers between devices  27.9 us (32%)
  Pallas kernels  20.5 us (23%)
    ppermute x2, waiting for transfers between devices, per_device(): lax.ppermute(fgram, ('tm', 'space'), hop(1, flip))  16.2 us
    ppermute x4, starting transfers between devices, per_device(): lax.ppermute(x, 'space', partner[k])  10.6 us
    ppermute x2, starting transfers between devices, per_device(): lax.ppermute(gram, ('tm', 'space'), hop(-1, flip))  10 us
    ppermute x4, waiting for transfers between devices, per_device(): lax.ppermute(x, 'space', partner[k])  9.26 us
    ppermute x3, waiting for transfers between devices, per_device(): lax.ppermute(gram, 'space', [(i, i ^ d) for i in range(peers)])  8.76 us
    pallas_call x1, Pallas kernels, interior(): pl.pallas_call(interior_kernel, out_shape=(vmem(K, NXL, NY, NZ), vmem(K,...  7.63 us
    pallas_call x2, Pallas kernels, edges(): pl.pallas_call(lambda *refs: edges_kernel(adjoint, *refs), out_shape=(vme...  6.66 us
    ppermute x2, waiting for transfers between devices, per_device(): lax.ppermute(gram, ('tm', 'space'), hop(-1, flip))  3.96 us
  transfers between devices with their start and end apart: 13, of which 7 were waited for; matrix products, arithmetic and copies ran while one was open for 0% of the time, Pallas kernels for 14%

profile of v1, /device:TPU:1, one launch (start us, length us, event | category | flops | bytes accessed | tf_op | source)
XLA Modules:
  0.0 87.3 jit_solution(7160050205705455081)
XLA Ops:
  0.6 1.8 %forward_pack.1 = (f32[10,3,32,128]{3,2,1,0:T(8,128)S(1)}, f32[10,3,32,128]{3,2,1,0:T(8,128)S(1)}) custom-call(f32[8,12,32,128]{3,2,1,0:T(8,128)} %bitcast.15, f32[4,12,32,128]{3,2,1,0:T(8,128)} %bitcast.7), custom_call_target="tpu_custom_call" | custom-call | tf_op jit(solution)/shard_map/forward_pack/pallas_call | solution.py:133
  2.4 8.9 %collective-permute-start = (f32[10,3,32,128]{3,2,1,0:T(8,128)S(1)}, f32[10,3,32,128]{3,2,1,0:T(8,128)S(1)}, u32[]{:S(2)}, u32[]{:S(2)}) collective-permute-start(f32[10,3,32,128]{3,2,1,0:T(8,128)S(1)} %get-tuple-element.25), channel_id=1, source_target_pairs={{0,15},{1,2},{2,1},{3,4},{4,3},{5,6},{6,5},{7,8},{8,7},{9,10},{10,... | collective-permute-start | bytes 1474568 | tf_op jit(solution)/shard_map/ppermute | solution.py:394
  11.4 0.0 collective-permute-start.1
  11.4 1.7 %adjoint_pack.1 = (f32[8,3,32,128]{3,2,1,0:T(8,128)S(1)}, f32[8,3,32,128]{3,2,1,0:T(8,128)S(1)}) custom-call(f32[8,12,32,128]{3,2,1,0:T(8,128)} %bitcast.12, f32[4,12,32,128]{3,2,1,0:T(8,128)} %bitcast.8), custom_call_target="tpu_custom_call" | custom-call | tf_op jit(solution)/shard_map/adjoint_pack/pallas_call | solution.py:133
  13.1 1.5 %collective-permute-start.3 = (f32[8,3,32,128]{3,2,1,0:T(8,128)S(1)}, f32[8,3,32,128]{3,2,1,0:T(8,128)S(1)}, u32[]{:S(2)}, u32[]{:S(2)}) collective-permute-start(f32[8,3,32,128]{3,2,1,0:T(8,128)S(1)} %get-tuple-element.31), channel_id=1, source_target_pairs={{0,15},{1,2},{2,1},{3,4},{4,3},{5,6},{6,5},{7,8},{8,7},{9,10},{10,... | collective-permute-start | bytes 1179656 | tf_op jit(solution)/shard_map/ppermute | solution.py:395
  14.6 0.1 collective-permute-start.4
  14.7 7.6 %interior.1 = (f32[8,12,32,128]{3,2,1,0:T(8,128)S(1)}, f32[8,12,32,128]{3,2,1,0:T(8,128)S(1)}, f32[4,8,2,32,128]{4,3,2,1,0:T(8,128)S(1)}, f32[4,8,2,32,128]{4,3,...) custom-call(f32[8,12,32,128]{3,2,1,0:T(8,128)} %bitcast.16, f32[8,12,32,128]{3,2,1,0:T(8,128)} %bitcast.13, ...), custom_call_target="tpu_custom_call" | custom-call | tf_op jit(solution)/shard_map/interior/pallas_call | solution.py:195
  22.4 8.4 %collective-permute-done.3.refs_7_ = f32[8,3,32,128]{3,2,1,0:T(8,128)S(1)} collective-permute-done((f32[8,3,32,128]{3,2,1,0:T(8,128)S(1)}, f32[8,3,32,128]{3,2,1,0:T(8,128)S(1)}, u32[]{:S(2)}, u32[]{:S(2)}) %collective-permute-start.3) | collective-permute-done | bytes 393248 | tf_op jit(solution)/shard_map/ppermute | solution.py:395
  30.7 0.9 %collective-permute-done.4.refs_8_ = f32[8,3,32,128]{3,2,1,0:T(8,128)S(1)} collective-permute-done((f32[8,3,32,128]{3,2,1,0:T(8,128)S(1)}, f32[8,3,32,128]{3,2,1,0:T(8,128)S(1)}, u32[]{:S(2)}, u32[]{:S(2)}) %collective-permute-start.4) | collective-permute-done | bytes 393248 | tf_op jit(solution)/shard_map/ppermute | solution.py:395
  31.6 0.0 collective-permute-done.refs_5_
  31.6 0.0 collective-permute-done.1.refs_6_
  31.6 3.4 %adjoint_edges.1 = (f32[8,12,32,128]{3,2,1,0:T(8,128)S(1)}, f32[40,128]{1,0:T(8,128)S(1)}) custom-call(f32[8,12,32,128]{3,2,1,0:T(8,128)} %bitcast.14, f32[4,12,32,128]{3,2,1,0:T(8,128)} %bitcast.10, f32[8,12,32,128]{3,2,1,0:T(8,128)S(1)} %get-tuple-element.28.refs_2_, ...), custom_call_target="tpu_custom_call", output_to_operand_aliasing={{0}: (2, {})} | custom-call | tf_op jit(solution)/shard_map/adjoint_edges/pallas_call | solution.py:287
  35.0 1.9 %collective-permute-start.5 = (f32[8,12,32,128]{3,2,1,0:T(8,128)S(1)}, f32[8,12,32,128]{3,2,1,0:T(8,128)S(1)}, u32[]{:S(2)}, u32[]{:S(2)}) collective-permute-start(f32[8,12,32,128]{3,2,1,0:T(8,128)S(1)} %get-tuple-element.33), channel_id=1, source_target_pairs={{16,0},{32,16},{48,32},{64,48},{80,64},{96,80},{112,96},{128,112},... | collective-permute-start | bytes 4718600 | tf_op jit(solution)/shard_map/ppermute | solution.py:402
  36.9 3.3 %forward_edges.1 = (f32[8,12,32,128]{3,2,1,0:T(8,128)S(1)}, f32[40,128]{1,0:T(8,128)S(1)}) custom-call(f32[8,12,32,128]{3,2,1,0:T(8,128)} %bitcast.17, f32[4,12,32,128]{3,2,1,0:T(8,128)} %bitcast.11, f32[8,12,32,128]{3,2,1,0:T(8,128)S(1)} %get-tuple-element.22.refs_2_, ...), custom_call_target="tpu_custom_call", output_to_operand_aliasing={{0}: (2, {})} | custom-call | tf_op jit(solution)/shard_map/forward_edges/pallas_call | solution.py:287
  40.2 1.3 %collective-permute-start.2 = (f32[8,12,32,128]{3,2,1,0:T(8,128)S(1)}, f32[8,12,32,128]{3,2,1,0:T(8,128)S(1)}, u32[]{:S(2)}, u32[]{:S(2)}) collective-permute-start(f32[8,12,32,128]{3,2,1,0:T(8,128)S(1)} %get-tuple-element.27), channel_id=1, source_target_pairs={{0,16},{16,32},{32,48},{48,64},{64,80},{80,96},{96,112},{112,128},... | collective-permute-start | bytes 4718600 | tf_op jit(solution)/shard_map/ppermute | solution.py:401
  41.5 0.5 collective-permute-start.6
  41.9 1.1 %collective-permute-start.7 = (f32[40,128]{1,0:T(8,128)S(1)}, f32[40,128]{1,0:T(8,128)S(1)}, u32[]{:S(2)}, u32[]{:S(2)}) collective-permute-start(f32[40,128]{1,0:T(8,128)S(1)} %get-tuple-element.34), channel_id=1, source_target_pairs={{0,24},{1,25},{2,26},{3,27},{4,28},{5,29},{6,30},{7,31},{8,16},{9,... | collective-permute-start | bytes 61448 | tf_op jit(solution)/shard_map/ppermute | solution.py:399
  43.1 16.2 %collective-permute-done.6 = f32[40,128]{1,0:T(8,128)S(1)} collective-permute-done((f32[40,128]{1,0:T(8,128)S(1)}, f32[40,128]{1,0:T(8,128)S(1)}, u32[]{:S(2)}, u32[]{:S(2)}) %collective-permute-start.6) | collective-permute-done | bytes 20512 | tf_op jit(solution)/shard_map/ppermute | solution.py:399
  59.3 0.0 collective-permute-done.7
  59.3 0.1 collective-permute-start.8
  59.4 3.1 %collective-permute-done.8 = f32[80,128]{1,0:T(8,128)S(1)} collective-permute-done((f32[80,128]{1,0:T(8,128)S(1)}, f32[80,128]{1,0:T(8,128)S(1)}, u32[]{:S(2)}, u32[]{:S(2)}) %collective-permute-start.8) | collective-permute-done | bytes 40992 | tf_op jit(solution)/shard_map/ppermute | solution.py:405
  62.5 0.0 collective-permute-start.9
  62.5 3.9 %collective-permute-done.9 = f32[80,128]{1,0:T(8,128)S(1)} collective-permute-done((f32[80,128]{1,0:T(8,128)S(1)}, f32[80,128]{1,0:T(8,128)S(1)}, u32[]{:S(2)}, u32[]{:S(2)}) %collective-permute-start.9) | collective-permute-done | bytes 40992 | tf_op jit(solution)/shard_map/ppermute | solution.py:405
  66.4 2.3 %collective-permute-start.10 = (f32[80,128]{1,0:T(8,128)S(1)}, f32[80,128]{1,0:T(8,128)S(1)}, u32[]{:S(2)}, u32[]{:S(2)}) collective-permute-start(f32[80,128]{1,0:T(8,128)S(1)} %add.14), channel_id=1, source_target_pairs={{0,7},{1,6},{2,5},{3,4},{4,3},{5,2},{6,1},{7,0},{8,15},{9,14},{10,... | collective-permute-start | bytes 122888 | tf_op jit(solution)/shard_map/ppermute | solution.py:405
  68.8 1.7 %collective-permute-done.10 = f32[80,128]{1,0:T(8,128)S(1)} collective-permute-done((f32[80,128]{1,0:T(8,128)S(1)}, f32[80,128]{1,0:T(8,128)S(1)}, u32[]{:S(2)}, u32[]{:S(2)}) %collective-permute-start.10) | collective-permute-done | bytes 40992 | tf_op jit(solution)/shard_map/ppermute | solution.py:405
  70.5 8.2 %collective-permute-start.11 = (f32[80,128]{1,0:T(8,128)S(1)}, f32[80,128]{1,0:T(8,128)S(1)}, u32[]{:S(2)}, u32[]{:S(2)}) collective-permute-start(f32[80,128]{1,0:T(8,128)S(1)} %add.15.gf), channel_id=1, source_target_pairs={{0,240},{1,241},{2,242},{3,243},{4,244},{5,245},{6,246},{7,247},{8... | collective-permute-start | bytes 122888 | tf_op jit(solution)/shard_map/ppermute | solution.py:406
  78.7 1.9 %collective-permute-start.12 = (f32[80,128]{1,0:T(8,128)S(1)}, f32[80,128]{1,0:T(8,128)S(1)}, u32[]{:S(2)}, u32[]{:S(2)}) collective-permute-start(f32[80,128]{1,0:T(8,128)S(1)} %add.15.gf), channel_id=1, source_target_pairs={{0,248},{1,249},{2,250},{3,251},{4,252},{5,253},{6,254},{7,255},{8... | collective-permute-start | bytes 122888 | tf_op jit(solution)/shard_map/ppermute | solution.py:406
  80.5 0.0 collective-permute-done.11.g0
  80.6 4.0 %collective-permute-done.12.g1 = f32[80,128]{1,0:T(8,128)S(1)} collective-permute-done((f32[80,128]{1,0:T(8,128)S(1)}, f32[80,128]{1,0:T(8,128)S(1)}, u32[]{:S(2)}, u32[]{:S(2)}) %collective-permute-start.12) | collective-permute-done | bytes 40992 | tf_op jit(solution)/shard_map/ppermute | solution.py:406
  84.5 0.0 collective-permute-done.5.ain
  84.5 0.0 collective-permute-done.2.fin
  84.5 2.8 %finish.1 = (f32[8,12,32,128]{3,2,1,0:T(8,128)}, f32[8,12,32,128]{3,2,1,0:T(8,128)}, f32[8,8]{1,0:T(8,128)}, f32[8,8]{1,0:T(8,128)}) custom-call(f32[8,12,32,128]{3,2,1,0:T(8,128)S(1)} %collective-permute-done.2.fin, f32[8,12,32,128]{3,2,1,0:T(8,128)S(1)} %collective-permute-done.5.ain, f32[80,128]{1,0:T(8,128)S(1)} %add.15.gf, ...), custom_call_target="tpu_custom_call" | custom-call | tf_op jit(solution)/shard_map/finish/pallas_call | solution.py:363
  (5 shorter events, 0.0 us)
Async XLA Ops:
  2.4 29.2 %collective-permute-start = (f32[10,3,32,128]{3,2,1,0:T(8,128)S(1)}, f32[10,3,32,128]{3,2,1,0:T(8,128)S(1)}, u32[]{:S(2)}, u32[]{:S(2)}) collective-permute-start(f32[10,3,32,128]{3,2,1,0:T(8,128)S(1)} %get-tuple-element.25), channel_id=1, source_target_pairs={{0,15},{1,2},{2,1},{3,4},{4,3},{5,6},{6,5},{7,8},{8,7},{9,10},{10,... | collective-permute-start | bytes 1474568 | tf_op jit(solution)/shard_map/ppermute | solution.py:394
  11.4 20.3 %collective-permute-start.1 = (f32[10,3,32,128]{3,2,1,0:T(8,128)S(1)}, f32[10,3,32,128]{3,2,1,0:T(8,128)S(1)}, u32[]{:S(2)}, u32[]{:S(2)}) collective-permute-start(f32[10,3,32,128]{3,2,1,0:T(8,128)S(1)} %get-tuple-element.26), channel_id=1, source_target_pairs={{0,1},{1,0},{2,3},{3,2},{4,5},{5,4},{6,7},{7,6},{8,9},{9,8},{10,11... | collective-permute-start | bytes 1474568 | tf_op jit(solution)/shard_map/ppermute | solution.py:394
  13.1 17.6 %collective-permute-start.3 = (f32[8,3,32,128]{3,2,1,0:T(8,128)S(1)}, f32[8,3,32,128]{3,2,1,0:T(8,128)S(1)}, u32[]{:S(2)}, u32[]{:S(2)}) collective-permute-start(f32[8,3,32,128]{3,2,1,0:T(8,128)S(1)} %get-tuple-element.31), channel_id=1, source_target_pairs={{0,15},{1,2},{2,1},{3,4},{4,3},{5,6},{6,5},{7,8},{8,7},{9,10},{10,... | collective-permute-start | bytes 1179656 | tf_op jit(solution)/shard_map/ppermute | solution.py:395
  14.6 17.0 %collective-permute-start.4 = (f32[8,3,32,128]{3,2,1,0:T(8,128)S(1)}, f32[8,3,32,128]{3,2,1,0:T(8,128)S(1)}, u32[]{:S(2)}, u32[]{:S(2)}) collective-permute-start(f32[8,3,32,128]{3,2,1,0:T(8,128)S(1)} %get-tuple-element.32), channel_id=1, source_target_pairs={{0,1},{1,0},{2,3},{3,2},{4,5},{5,4},{6,7},{7,6},{8,9},{9,8},{10,11... | collective-permute-start | bytes 1179656 | tf_op jit(solution)/shard_map/ppermute | solution.py:395
  35.0 49.5 %collective-permute-start.5 = (f32[8,12,32,128]{3,2,1,0:T(8,128)S(1)}, f32[8,12,32,128]{3,2,1,0:T(8,128)S(1)}, u32[]{:S(2)}, u32[]{:S(2)}) collective-permute-start(f32[8,12,32,128]{3,2,1,0:T(8,128)S(1)} %get-tuple-element.33), channel_id=1, source_target_pairs={{16,0},{32,16},{48,32},{64,48},{80,64},{96,80},{112,96},{128,112},... | collective-permute-start | bytes 4718600 | tf_op jit(solution)/shard_map/ppermute | solution.py:402
  40.2 44.3 %collective-permute-start.2 = (f32[8,12,32,128]{3,2,1,0:T(8,128)S(1)}, f32[8,12,32,128]{3,2,1,0:T(8,128)S(1)}, u32[]{:S(2)}, u32[]{:S(2)}) collective-permute-start(f32[8,12,32,128]{3,2,1,0:T(8,128)S(1)} %get-tuple-element.27), channel_id=1, source_target_pairs={{0,16},{16,32},{32,48},{48,64},{64,80},{80,96},{96,112},{112,128},... | collective-permute-start | bytes 4718600 | tf_op jit(solution)/shard_map/ppermute | solution.py:401
  41.5 17.8 %collective-permute-start.6 = (f32[40,128]{1,0:T(8,128)S(1)}, f32[40,128]{1,0:T(8,128)S(1)}, u32[]{:S(2)}, u32[]{:S(2)}) collective-permute-start(f32[40,128]{1,0:T(8,128)S(1)} %get-tuple-element.34), channel_id=1, source_target_pairs={{0,16},{1,17},{2,18},{3,19},{4,20},{5,21},{6,22},{7,23},{8,24},{9,... | collective-permute-start | bytes 61448 | tf_op jit(solution)/shard_map/ppermute | solution.py:399
  41.9 17.3 %collective-permute-start.7 = (f32[40,128]{1,0:T(8,128)S(1)}, f32[40,128]{1,0:T(8,128)S(1)}, u32[]{:S(2)}, u32[]{:S(2)}) collective-permute-start(f32[40,128]{1,0:T(8,128)S(1)} %get-tuple-element.34), channel_id=1, source_target_pairs={{0,24},{1,25},{2,26},{3,27},{4,28},{5,29},{6,30},{7,31},{8,16},{9,... | collective-permute-start | bytes 61448 | tf_op jit(solution)/shard_map/ppermute | solution.py:399
  59.3 3.2 %collective-permute-start.8 = (f32[80,128]{1,0:T(8,128)S(1)}, f32[80,128]{1,0:T(8,128)S(1)}, u32[]{:S(2)}, u32[]{:S(2)}) collective-permute-start(f32[80,128]{1,0:T(8,128)S(1)} %pad_maximum_fusion), channel_id=1, source_target_pairs={{0,1},{1,0},{2,3},{3,2},{4,5},{5,4},{6,7},{7,6},{8,9},{9,8},{10,11... | collective-permute-start | bytes 122888 | tf_op jit(solution)/shard_map/ppermute | solution.py:405
  62.5 3.9 %collective-permute-start.9 = (f32[80,128]{1,0:T(8,128)S(1)}, f32[80,128]{1,0:T(8,128)S(1)}, u32[]{:S(2)}, u32[]{:S(2)}) collective-permute-start(f32[80,128]{1,0:T(8,128)S(1)} %fusion), channel_id=1, source_target_pairs={{0,2},{1,3},{2,0},{3,1},{4,6},{5,7},{6,4},{7,5},{8,10},{9,11},{10,... | collective-permute-start | bytes 122888 | tf_op jit(solution)/shard_map/ppermute | solution.py:405
  66.4 4.1 %collective-permute-start.10 = (f32[80,128]{1,0:T(8,128)S(1)}, f32[80,128]{1,0:T(8,128)S(1)}, u32[]{:S(2)}, u32[]{:S(2)}) collective-permute-start(f32[80,128]{1,0:T(8,128)S(1)} %add.14), channel_id=1, source_target_pairs={{0,7},{1,6},{2,5},{3,4},{4,3},{5,2},{6,1},{7,0},{8,15},{9,14},{10,... | collective-permute-start | bytes 122888 | tf_op jit(solution)/shard_map/ppermute | solution.py:405
  70.5 10.0 %collective-permute-start.11 = (f32[80,128]{1,0:T(8,128)S(1)}, f32[80,128]{1,0:T(8,128)S(1)}, u32[]{:S(2)}, u32[]{:S(2)}) collective-permute-start(f32[80,128]{1,0:T(8,128)S(1)} %add.15.gf), channel_id=1, source_target_pairs={{0,240},{1,241},{2,242},{3,243},{4,244},{5,245},{6,246},{7,247},{8... | collective-permute-start | bytes 122888 | tf_op jit(solution)/shard_map/ppermute | solution.py:406
  78.7 5.8 %collective-permute-start.12 = (f32[80,128]{1,0:T(8,128)S(1)}, f32[80,128]{1,0:T(8,128)S(1)}, u32[]{:S(2)}, u32[]{:S(2)}) collective-permute-start(f32[80,128]{1,0:T(8,128)S(1)} %add.15.gf), channel_id=1, source_target_pairs={{0,248},{1,249},{2,250},{3,251},{4,252},{5,253},{6,254},{7,255},{8... | collective-permute-start | bytes 122888 | tf_op jit(solution)/shard_map/ppermute | solution.py:406

commit v2 on v1

--- a/solution.py
+++ b/solution.py
@@ -269,15 +269,14 @@
                 )
             return carry
 
-        lax.fori_loop(0, 2, body, 0)
+        for side in range(2):
+            body(side, 0)
         if stage == 1:
             wait(later)
 
-    def body(side, carry):
-        add_gram(gram, [lambda f, t, p=side * 9 + j: block[f, p, pl.ds(8 * t, 8)] for j in range(3)])
-        return carry
-
-    lax.fori_loop(0, 2, body, 0)
+    for side in range(2):
+        base = side * (NXL - 3)
+        add_gram(gram, [lambda f, t, p=base + j: block[f, p, pl.ds(8 * t, 8)] for j in range(3)])
     gout[pl.ds(0, NP)] = jnp.sum(gram[...], axis=1) * (1.0 / (NXL * NY * NZ * 16))
     gout[pl.ds(NP, GROWS - NP)] = jnp.zeros((GROWS - NP, NZ), F32)
 

time: 87.5 us -> 86.8 us (level)
  no operation moved by 1% of the time
where the time goes in v2:
time: 86.8 us; the launch traced here: 86.6 us
  waiting for transfers between devices  37.8 us (44%)
  starting transfers between devices  28.2 us (32%)
  Pallas kernels  19.7 us (23%)
    ppermute x2, waiting for transfers between devices, per_device(): lax.ppermute(fgram, ('tm', 'space'), hop(1, flip))  16.2 us
    ppermute x4, starting transfers between devices, per_device(): lax.ppermute(x, 'space', partner[k])  10.6 us
    ppermute x2, starting transfers between devices, per_device(): lax.ppermute(gram, ('tm', 'space'), hop(-1, flip))  9.88 us
    ppermute x4, waiting for transfers between devices, per_device(): lax.ppermute(x, 'space', partner[k])  9.26 us
    ppermute x3, waiting for transfers between devices, per_device(): lax.ppermute(gram, 'space', [(i, i ^ d) for i in range(peers)])  8.43 us
    pallas_call x1, Pallas kernels, interior(): pl.pallas_call(interior_kernel, out_shape=(vmem(K, NXL, NY, NZ), vmem(K,...  7.63 us
    pallas_call x2, Pallas kernels, edges(): pl.pallas_call(lambda *refs: edges_kernel(adjoint, *refs), out_shape=(vme...  5.78 us
    ppermute x2, waiting for transfers between devices, per_device(): lax.ppermute(gram, ('tm', 'space'), hop(-1, flip))  3.97 us
  transfers between devices with their start and end apart: 13, of which 7 were waited for; matrix products, arithmetic and copies ran while one was open for 0% of the time, Pallas kernels for 14%

profile of v2, /device:TPU:1, one launch (start us, length us, event | category | flops | bytes accessed | tf_op | source)
XLA Modules:
  0.0 86.6 jit_solution(6994543095602686855)
XLA Ops:
  0.6 1.8 %forward_pack.1 = (f32[10,3,32,128]{3,2,1,0:T(8,128)S(1)}, f32[10,3,32,128]{3,2,1,0:T(8,128)S(1)}) custom-call(f32[8,12,32,128]{3,2,1,0:T(8,128)} %bitcast.15, f32[4,12,32,128]{3,2,1,0:T(8,128)} %bitcast.7), custom_call_target="tpu_custom_call" | custom-call | tf_op jit(solution)/shard_map/forward_pack/pallas_call | solution.py:133
  2.4 8.9 %collective-permute-start = (f32[10,3,32,128]{3,2,1,0:T(8,128)S(1)}, f32[10,3,32,128]{3,2,1,0:T(8,128)S(1)}, u32[]{:S(2)}, u32[]{:S(2)}) collective-permute-start(f32[10,3,32,128]{3,2,1,0:T(8,128)S(1)} %get-tuple-element.25), channel_id=1, source_target_pairs={{0,15},{1,2},{2,1},{3,4},{4,3},{5,6},{6,5},{7,8},{8,7},{9,10},{10,... | collective-permute-start | bytes 1474568 | tf_op jit(solution)/shard_map/ppermute | solution.py:393
  11.4 0.0 collective-permute-start.1
  11.4 1.7 %adjoint_pack.1 = (f32[8,3,32,128]{3,2,1,0:T(8,128)S(1)}, f32[8,3,32,128]{3,2,1,0:T(8,128)S(1)}) custom-call(f32[8,12,32,128]{3,2,1,0:T(8,128)} %bitcast.12, f32[4,12,32,128]{3,2,1,0:T(8,128)} %bitcast.8), custom_call_target="tpu_custom_call" | custom-call | tf_op jit(solution)/shard_map/adjoint_pack/pallas_call | solution.py:133
  13.1 1.5 %collective-permute-start.3 = (f32[8,3,32,128]{3,2,1,0:T(8,128)S(1)}, f32[8,3,32,128]{3,2,1,0:T(8,128)S(1)}, u32[]{:S(2)}, u32[]{:S(2)}) collective-permute-start(f32[8,3,32,128]{3,2,1,0:T(8,128)S(1)} %get-tuple-element.31), channel_id=1, source_target_pairs={{0,15},{1,2},{2,1},{3,4},{4,3},{5,6},{6,5},{7,8},{8,7},{9,10},{10,... | collective-permute-start | bytes 1179656 | tf_op jit(solution)/shard_map/ppermute | solution.py:394
  14.6 0.1 collective-permute-start.4
  14.7 7.6 %interior.1 = (f32[8,12,32,128]{3,2,1,0:T(8,128)S(1)}, f32[8,12,32,128]{3,2,1,0:T(8,128)S(1)}, f32[4,8,2,32,128]{4,3,2,1,0:T(8,128)S(1)}, f32[4,8,2,32,128]{4,3,...) custom-call(f32[8,12,32,128]{3,2,1,0:T(8,128)} %bitcast.16, f32[8,12,32,128]{3,2,1,0:T(8,128)} %bitcast.13, ...), custom_call_target="tpu_custom_call" | custom-call | tf_op jit(solution)/shard_map/interior/pallas_call | solution.py:195
  22.4 8.4 %collective-permute-done.3.refs_7_ = f32[8,3,32,128]{3,2,1,0:T(8,128)S(1)} collective-permute-done((f32[8,3,32,128]{3,2,1,0:T(8,128)S(1)}, f32[8,3,32,128]{3,2,1,0:T(8,128)S(1)}, u32[]{:S(2)}, u32[]{:S(2)}) %collective-permute-start.3) | collective-permute-done | bytes 393248 | tf_op jit(solution)/shard_map/ppermute | solution.py:394
  30.7 0.9 %collective-permute-done.4.refs_8_ = f32[8,3,32,128]{3,2,1,0:T(8,128)S(1)} collective-permute-done((f32[8,3,32,128]{3,2,1,0:T(8,128)S(1)}, f32[8,3,32,128]{3,2,1,0:T(8,128)S(1)}, u32[]{:S(2)}, u32[]{:S(2)}) %collective-permute-start.4) | collective-permute-done | bytes 393248 | tf_op jit(solution)/shard_map/ppermute | solution.py:394
  31.6 0.0 collective-permute-done.refs_5_
  31.6 0.0 collective-permute-done.1.refs_6_
  31.6 2.9 %adjoint_edges.1 = (f32[8,12,32,128]{3,2,1,0:T(8,128)S(1)}, f32[40,128]{1,0:T(8,128)S(1)}) custom-call(f32[8,12,32,128]{3,2,1,0:T(8,128)} %bitcast.14, f32[4,12,32,128]{3,2,1,0:T(8,128)} %bitcast.10, f32[8,12,32,128]{3,2,1,0:T(8,128)S(1)} %get-tuple-element.28.refs_2_, ...), custom_call_target="tpu_custom_call", output_to_operand_aliasing={{0}: (2, {})} | custom-call | tf_op jit(solution)/shard_map/adjoint_edges/pallas_call | solution.py:286
  34.6 1.9 %collective-permute-start.5 = (f32[8,12,32,128]{3,2,1,0:T(8,128)S(1)}, f32[8,12,32,128]{3,2,1,0:T(8,128)S(1)}, u32[]{:S(2)}, u32[]{:S(2)}) collective-permute-start(f32[8,12,32,128]{3,2,1,0:T(8,128)S(1)} %get-tuple-element.33), channel_id=1, source_target_pairs={{16,0},{32,16},{48,32},{64,48},{80,64},{96,80},{112,96},{128,112},... | collective-permute-start | bytes 4718600 | tf_op jit(solution)/shard_map/ppermute | solution.py:401
  36.5 2.8 %forward_edges.1 = (f32[8,12,32,128]{3,2,1,0:T(8,128)S(1)}, f32[40,128]{1,0:T(8,128)S(1)}) custom-call(f32[8,12,32,128]{3,2,1,0:T(8,128)} %bitcast.17, f32[4,12,32,128]{3,2,1,0:T(8,128)} %bitcast.11, f32[8,12,32,128]{3,2,1,0:T(8,128)S(1)} %get-tuple-element.22.refs_2_, ...), custom_call_target="tpu_custom_call", output_to_operand_aliasing={{0}: (2, {})} | custom-call | tf_op jit(solution)/shard_map/forward_edges/pallas_call | solution.py:286
  39.3 1.3 %collective-permute-start.2 = (f32[8,12,32,128]{3,2,1,0:T(8,128)S(1)}, f32[8,12,32,128]{3,2,1,0:T(8,128)S(1)}, u32[]{:S(2)}, u32[]{:S(2)}) collective-permute-start(f32[8,12,32,128]{3,2,1,0:T(8,128)S(1)} %get-tuple-element.27), channel_id=1, source_target_pairs={{0,16},{16,32},{32,48},{48,64},{64,80},{80,96},{96,112},{112,128},... | collective-permute-start | bytes 4718600 | tf_op jit(solution)/shard_map/ppermute | solution.py:400
  40.6 0.5 collective-permute-start.6
  41.1 1.1 %collective-permute-start.7 = (f32[40,128]{1,0:T(8,128)S(1)}, f32[40,128]{1,0:T(8,128)S(1)}, u32[]{:S(2)}, u32[]{:S(2)}) collective-permute-start(f32[40,128]{1,0:T(8,128)S(1)} %get-tuple-element.34), channel_id=1, source_target_pairs={{0,24},{1,25},{2,26},{3,27},{4,28},{5,29},{6,30},{7,31},{8,16},{9,... | collective-permute-start | bytes 61448 | tf_op jit(solution)/shard_map/ppermute | solution.py:398
  42.2 16.2 %collective-permute-done.6 = f32[40,128]{1,0:T(8,128)S(1)} collective-permute-done((f32[40,128]{1,0:T(8,128)S(1)}, f32[40,128]{1,0:T(8,128)S(1)}, u32[]{:S(2)}, u32[]{:S(2)}) %collective-permute-start.6) | collective-permute-done | bytes 20512 | tf_op jit(solution)/shard_map/ppermute | solution.py:398
  58.4 0.0 collective-permute-done.7
  58.4 0.2 collective-permute-start.8
  58.6 3.0 %collective-permute-done.8 = f32[80,128]{1,0:T(8,128)S(1)} collective-permute-done((f32[80,128]{1,0:T(8,128)S(1)}, f32[80,128]{1,0:T(8,128)S(1)}, u32[]{:S(2)}, u32[]{:S(2)}) %collective-permute-start.8) | collective-permute-done | bytes 40992 | tf_op jit(solution)/shard_map/ppermute | solution.py:404
  61.6 0.0 collective-permute-start.9
  61.7 4.0 %collective-permute-done.9 = f32[80,128]{1,0:T(8,128)S(1)} collective-permute-done((f32[80,128]{1,0:T(8,128)S(1)}, f32[80,128]{1,0:T(8,128)S(1)}, u32[]{:S(2)}, u32[]{:S(2)}) %collective-permute-start.9) | collective-permute-done | bytes 40992 | tf_op jit(solution)/shard_map/ppermute | solution.py:404
  65.7 2.7 %collective-permute-start.10 = (f32[80,128]{1,0:T(8,128)S(1)}, f32[80,128]{1,0:T(8,128)S(1)}, u32[]{:S(2)}, u32[]{:S(2)}) collective-permute-start(f32[80,128]{1,0:T(8,128)S(1)} %add.14), channel_id=1, source_target_pairs={{0,7},{1,6},{2,5},{3,4},{4,3},{5,2},{6,1},{7,0},{8,15},{9,14},{10,... | collective-permute-start | bytes 122888 | tf_op jit(solution)/shard_map/ppermute | solution.py:404
  68.4 1.4 %collective-permute-done.10 = f32[80,128]{1,0:T(8,128)S(1)} collective-permute-done((f32[80,128]{1,0:T(8,128)S(1)}, f32[80,128]{1,0:T(8,128)S(1)}, u32[]{:S(2)}, u32[]{:S(2)}) %collective-permute-start.10) | collective-permute-done | bytes 40992 | tf_op jit(solution)/shard_map/ppermute | solution.py:404
  69.8 8.0 %collective-permute-start.11 = (f32[80,128]{1,0:T(8,128)S(1)}, f32[80,128]{1,0:T(8,128)S(1)}, u32[]{:S(2)}, u32[]{:S(2)}) collective-permute-start(f32[80,128]{1,0:T(8,128)S(1)} %add.15.gf), channel_id=1, source_target_pairs={{0,240},{1,241},{2,242},{3,243},{4,244},{5,245},{6,246},{7,247},{8... | collective-permute-start | bytes 122888 | tf_op jit(solution)/shard_map/ppermute | solution.py:405
  77.8 1.9 %collective-permute-start.12 = (f32[80,128]{1,0:T(8,128)S(1)}, f32[80,128]{1,0:T(8,128)S(1)}, u32[]{:S(2)}, u32[]{:S(2)}) collective-permute-start(f32[80,128]{1,0:T(8,128)S(1)} %add.15.gf), channel_id=1, source_target_pairs={{0,248},{1,249},{2,250},{3,251},{4,252},{5,253},{6,254},{7,255},{8... | collective-permute-start | bytes 122888 | tf_op jit(solution)/shard_map/ppermute | solution.py:405
  79.7 0.0 collective-permute-done.11.g0
  79.7 4.0 %collective-permute-done.12.g1 = f32[80,128]{1,0:T(8,128)S(1)} collective-permute-done((f32[80,128]{1,0:T(8,128)S(1)}, f32[80,128]{1,0:T(8,128)S(1)}, u32[]{:S(2)}, u32[]{:S(2)}) %collective-permute-start.12) | collective-permute-done | bytes 40992 | tf_op jit(solution)/shard_map/ppermute | solution.py:405
  83.6 0.0 collective-permute-done.5.ain
  83.6 0.0 collective-permute-done.2.fin
  83.7 2.8 %finish.1 = (f32[8,12,32,128]{3,2,1,0:T(8,128)}, f32[8,12,32,128]{3,2,1,0:T(8,128)}, f32[8,8]{1,0:T(8,128)}, f32[8,8]{1,0:T(8,128)}) custom-call(f32[8,12,32,128]{3,2,1,0:T(8,128)S(1)} %collective-permute-done.2.fin, f32[8,12,32,128]{3,2,1,0:T(8,128)S(1)} %collective-permute-done.5.ain, f32[80,128]{1,0:T(8,128)S(1)} %add.15.gf, ...), custom_call_target="tpu_custom_call" | custom-call | tf_op jit(solution)/shard_map/finish/pallas_call | solution.py:362
  (5 shorter events, 0.0 us)
Async XLA Ops:
  2.4 29.2 %collective-permute-start = (f32[10,3,32,128]{3,2,1,0:T(8,128)S(1)}, f32[10,3,32,128]{3,2,1,0:T(8,128)S(1)}, u32[]{:S(2)}, u32[]{:S(2)}) collective-permute-start(f32[10,3,32,128]{3,2,1,0:T(8,128)S(1)} %get-tuple-element.25), channel_id=1, source_target_pairs={{0,15},{1,2},{2,1},{3,4},{4,3},{5,6},{6,5},{7,8},{8,7},{9,10},{10,... | collective-permute-start | bytes 1474568 | tf_op jit(solution)/shard_map/ppermute | solution.py:393
  11.4 20.3 %collective-permute-start.1 = (f32[10,3,32,128]{3,2,1,0:T(8,128)S(1)}, f32[10,3,32,128]{3,2,1,0:T(8,128)S(1)}, u32[]{:S(2)}, u32[]{:S(2)}) collective-permute-start(f32[10,3,32,128]{3,2,1,0:T(8,128)S(1)} %get-tuple-element.26), channel_id=1, source_target_pairs={{0,1},{1,0},{2,3},{3,2},{4,5},{5,4},{6,7},{7,6},{8,9},{9,8},{10,11... | collective-permute-start | bytes 1474568 | tf_op jit(solution)/shard_map/ppermute | solution.py:393
  13.1 17.6 %collective-permute-start.3 = (f32[8,3,32,128]{3,2,1,0:T(8,128)S(1)}, f32[8,3,32,128]{3,2,1,0:T(8,128)S(1)}, u32[]{:S(2)}, u32[]{:S(2)}) collective-permute-start(f32[8,3,32,128]{3,2,1,0:T(8,128)S(1)} %get-tuple-element.31), channel_id=1, source_target_pairs={{0,15},{1,2},{2,1},{3,4},{4,3},{5,6},{6,5},{7,8},{8,7},{9,10},{10,... | collective-permute-start | bytes 1179656 | tf_op jit(solution)/shard_map/ppermute | solution.py:394
  14.6 17.0 %collective-permute-start.4 = (f32[8,3,32,128]{3,2,1,0:T(8,128)S(1)}, f32[8,3,32,128]{3,2,1,0:T(8,128)S(1)}, u32[]{:S(2)}, u32[]{:S(2)}) collective-permute-start(f32[8,3,32,128]{3,2,1,0:T(8,128)S(1)} %get-tuple-element.32), channel_id=1, source_target_pairs={{0,1},{1,0},{2,3},{3,2},{4,5},{5,4},{6,7},{7,6},{8,9},{9,8},{10,11... | collective-permute-start | bytes 1179656 | tf_op jit(solution)/shard_map/ppermute | solution.py:394
  34.6 49.1 %collective-permute-start.5 = (f32[8,12,32,128]{3,2,1,0:T(8,128)S(1)}, f32[8,12,32,128]{3,2,1,0:T(8,128)S(1)}, u32[]{:S(2)}, u32[]{:S(2)}) collective-permute-start(f32[8,12,32,128]{3,2,1,0:T(8,128)S(1)} %get-tuple-element.33), channel_id=1, source_target_pairs={{16,0},{32,16},{48,32},{64,48},{80,64},{96,80},{112,96},{128,112},... | collective-permute-start | bytes 4718600 | tf_op jit(solution)/shard_map/ppermute | solution.py:401
  39.3 44.3 %collective-permute-start.2 = (f32[8,12,32,128]{3,2,1,0:T(8,128)S(1)}, f32[8,12,32,128]{3,2,1,0:T(8,128)S(1)}, u32[]{:S(2)}, u32[]{:S(2)}) collective-permute-start(f32[8,12,32,128]{3,2,1,0:T(8,128)S(1)} %get-tuple-element.27), channel_id=1, source_target_pairs={{0,16},{16,32},{32,48},{48,64},{64,80},{80,96},{96,112},{112,128},... | collective-permute-start | bytes 4718600 | tf_op jit(solution)/shard_map/ppermute | solution.py:400
  40.6 17.8 %collective-permute-start.6 = (f32[40,128]{1,0:T(8,128)S(1)}, f32[40,128]{1,0:T(8,128)S(1)}, u32[]{:S(2)}, u32[]{:S(2)}) collective-permute-start(f32[40,128]{1,0:T(8,128)S(1)} %get-tuple-element.34), channel_id=1, source_target_pairs={{0,16},{1,17},{2,18},{3,19},{4,20},{5,21},{6,22},{7,23},{8,24},{9,... | collective-permute-start | bytes 61448 | tf_op jit(solution)/shard_map/ppermute | solution.py:398
  41.1 17.3 %collective-permute-start.7 = (f32[40,128]{1,0:T(8,128)S(1)}, f32[40,128]{1,0:T(8,128)S(1)}, u32[]{:S(2)}, u32[]{:S(2)}) collective-permute-start(f32[40,128]{1,0:T(8,128)S(1)} %get-tuple-element.34), channel_id=1, source_target_pairs={{0,24},{1,25},{2,26},{3,27},{4,28},{5,29},{6,30},{7,31},{8,16},{9,... | collective-permute-start | bytes 61448 | tf_op jit(solution)/shard_map/ppermute | solution.py:398
  58.4 3.2 %collective-permute-start.8 = (f32[80,128]{1,0:T(8,128)S(1)}, f32[80,128]{1,0:T(8,128)S(1)}, u32[]{:S(2)}, u32[]{:S(2)}) collective-permute-start(f32[80,128]{1,0:T(8,128)S(1)} %pad_maximum_fusion), channel_id=1, source_target_pairs={{0,1},{1,0},{2,3},{3,2},{4,5},{5,4},{6,7},{7,6},{8,9},{9,8},{10,11... | collective-permute-start | bytes 122888 | tf_op jit(solution)/shard_map/ppermute | solution.py:404
  61.6 4.0 %collective-permute-start.9 = (f32[80,128]{1,0:T(8,128)S(1)}, f32[80,128]{1,0:T(8,128)S(1)}, u32[]{:S(2)}, u32[]{:S(2)}) collective-permute-start(f32[80,128]{1,0:T(8,128)S(1)} %fusion), channel_id=1, source_target_pairs={{0,2},{1,3},{2,0},{3,1},{4,6},{5,7},{6,4},{7,5},{8,10},{9,11},{10,... | collective-permute-start | bytes 122888 | tf_op jit(solution)/shard_map/ppermute | solution.py:404
  65.7 4.1 %collective-permute-start.10 = (f32[80,128]{1,0:T(8,128)S(1)}, f32[80,128]{1,0:T(8,128)S(1)}, u32[]{:S(2)}, u32[]{:S(2)}) collective-permute-start(f32[80,128]{1,0:T(8,128)S(1)} %add.14), channel_id=1, source_target_pairs={{0,7},{1,6},{2,5},{3,4},{4,3},{5,2},{6,1},{7,0},{8,15},{9,14},{10,... | collective-permute-start | bytes 122888 | tf_op jit(solution)/shard_map/ppermute | solution.py:404
  69.8 9.9 %collective-permute-start.11 = (f32[80,128]{1,0:T(8,128)S(1)}, f32[80,128]{1,0:T(8,128)S(1)}, u32[]{:S(2)}, u32[]{:S(2)}) collective-permute-start(f32[80,128]{1,0:T(8,128)S(1)} %add.15.gf), channel_id=1, source_target_pairs={{0,240},{1,241},{2,242},{3,243},{4,244},{5,245},{6,246},{7,247},{8... | collective-permute-start | bytes 122888 | tf_op jit(solution)/shard_map/ppermute | solution.py:405
  77.8 5.8 %collective-permute-start.12 = (f32[80,128]{1,0:T(8,128)S(1)}, f32[80,128]{1,0:T(8,128)S(1)}, u32[]{:S(2)}, u32[]{:S(2)}) collective-permute-start(f32[80,128]{1,0:T(8,128)S(1)} %add.15.gf), channel_id=1, source_target_pairs={{0,248},{1,249},{2,250},{3,251},{4,252},{5,253},{6,254},{7,255},{8... | collective-permute-start | bytes 122888 | tf_op jit(solution)/shard_map/ppermute | solution.py:405
